TPU v7x, 256 devices: a whole 4x4x8 slice. The times are simulated.
256 devices in a mesh: section: 4 (over y), seq: 64 (over z, x, core).
Axes of the slice: x: 4, y: 4, z: 8, core: 2. Of those that a mesh axis runs over, the one named last changes fastest.
Arguments:
- span_inputs: bfloat16 [4, 2048, 3, 8192], P('section', 'seq'), may hold values from -28 to 28
- out_grad: bfloat16 [4, 2048, 8192], P('section', 'seq'), may hold values from -48 to 48
- past_cache: bfloat16 [4, 3072, 2, 64, 128], P('section', None, None, 'seq'), may hold values from -5 to 5
- past_accum: float32 [4, 3072, 2, 64, 128], P('section', None, None, 'seq'), may hold values from -0.6 to 0.6
- offsets: int32 [4], P('section'), may hold values from 0 to 3072, as said below
- lengths: int32 [4], P('section'), may hold values from 1024 to 2048, as said below
Outputs:
- next_grads: bfloat16 [4, 2048, 3, 8192], P('section', 'seq')
- new_accum: float32 [4, 3072, 2, 64, 128], P('section', None, None, 'seq')
Inputs may be any that keep to these rules, and one draw needn't show every extreme that they name: The first offsets[s] rows of past_cache[s] and past_accum[s] belong to the sequence; one section's offset is 3072. Rows of a span from lengths[s] on are padding; one section's length is 2048.
All inputs are finite; a program needn't handle non-finite values.
Results may differ from a plain program's by a relative error of at most 0.0068.
Values may be sent and summed in bfloat16 or wider, within the bound.
No kernel may reach another device: no remote copies, remote signals or barrier semaphores. Data moves between devices by JAX's collectives and lax.ppermute only.
A program may use at most 128 MiB of HBM per device.

v0:
```python
import math
import jax
import jax.numpy as jnp
from jax import lax
from jax.sharding import PartitionSpec as P

HEADS = 64
DH = 128


def from_behind(block, axis, distance):
    devices = range(lax.axis_size(axis))
    route = [((i - distance) % len(devices), i) for i in devices]
    return lax.ppermute(block, axis, route)


def per_device(span_inputs, out_grad, past_cache, past_accum, offsets, lengths):
    scale_factor = 1.0 / math.sqrt(DH)
    tok_rows = span_inputs.shape[1]
    local_rows = span_inputs[0].reshape(tok_rows, 3, HEADS, DH)
    upstream = out_grad[0].reshape(tok_rows, 1, HEADS, DH)
    offset = offsets[0]
    length = lengths[0]
    cached = past_cache[0]
    past_len = cached.shape[0]
    head_inputs, head_dout = (
        lax.all_to_all(local_rows, "seq", split_axis=2, concat_axis=0, tiled=True),
        lax.all_to_all(upstream, "seq", split_axis=2, concat_axis=0, tiled=True),
    )
    span_len = head_inputs.shape[0]
    local_heads = head_inputs.shape[2]
    block_rows = min(512, span_len)
    block_count = span_len // block_rows
    all_keys = jnp.concatenate([cached[:, 0], head_inputs[:, 1]], axis=0)
    all_values = jnp.concatenate([cached[:, 1], head_inputs[:, 2]], axis=0)
    key_count = all_keys.shape[0]
    queries = head_inputs[:, 0].reshape(block_count, block_rows, local_heads, DH)
    starts = jnp.arange(block_count, dtype=jnp.int32) * block_rows
    key_index = jnp.arange(key_count, dtype=jnp.int32)
    in_span = key_index - past_len

    def scores(query_block, start):
        query_pos = start + jnp.arange(block_rows, dtype=jnp.int32)
        visible = jnp.where(
            key_index[None, :] < past_len,
            key_index[None, :] < offset,
            (in_span[None, :] <= query_pos[:, None]) & (in_span[None, :] < length),
        )
        raw_scores = (
            jnp.einsum("qhd,khd->hqk", query_block, all_keys, preferred_element_type=jnp.float32)
            * scale_factor
        )
        return jnp.where(visible[None], raw_scores, -jnp.inf)

    def backward_block(running, query_block, dout_block, masked):
        grad_keys, grad_values = running
        row_max = jnp.max(masked, axis=-1, keepdims=True)
        exp_terms = jnp.exp(masked - row_max)
        attention = exp_terms / jnp.sum(exp_terms, axis=-1, keepdims=True)
        attention_low = attention.astype(jnp.bfloat16)
        dprobs = jnp.einsum(
            "qhd,khd->hqk", dout_block, all_values, preferred_element_type=jnp.float32
        )
        row_delta = jnp.sum(attention * dprobs, axis=-1, keepdims=True)
        dscores = (attention * (dprobs - row_delta)).astype(jnp.bfloat16)
        grad_query = (
            jnp.einsum("hqk,khd->qhd", dscores, all_keys, preferred_element_type=jnp.float32)
            * scale_factor
        ).astype(jnp.bfloat16)
        grad_keys = (
            grad_keys
            + jnp.einsum("hqk,qhd->khd", dscores, query_block, preferred_element_type=jnp.float32)
            * scale_factor
        )
        grad_values = grad_values + jnp.einsum(
            "hqk,qhd->khd", attention_low, dout_block, preferred_element_type=jnp.float32
        )
        return ((grad_keys, grad_values), grad_query)

    zero_grads = (
        jnp.zeros((key_count, local_heads, DH), jnp.float32),
        jnp.zeros((key_count, local_heads, DH), jnp.float32),
    )
    rows_index = jnp.arange(span_len, dtype=jnp.int32)
    cleared = jnp.where(
        (rows_index < length)[:, None, None], head_dout[:, 0], jnp.zeros((), jnp.bfloat16)
    )
    dout_blocks = cleared.reshape(block_count, block_rows, local_heads, DH)

    def scan_step(running, scan_items):
        query_block, dout_block, start = scan_items
        return backward_block(running, query_block, dout_block, scores(query_block, start))

    (grad_keys, grad_values), grad_query = lax.scan(
        scan_step, zero_grads, (queries, dout_blocks, starts)
    )
    new_accum = past_accum[0] + jnp.stack([grad_keys[:past_len], grad_values[:past_len]], axis=1)
    span_grads = jnp.stack(
        [
            grad_query.reshape(span_len, local_heads, DH),
            grad_keys[past_len:].astype(jnp.bfloat16),
            grad_values[past_len:].astype(jnp.bfloat16),
        ],
        axis=1,
    )
    regrouped = lax.all_to_all(span_grads, "seq", split_axis=0, concat_axis=2, tiled=True)
    moved = from_behind(regrouped, "section", -1)
    return (moved.reshape(1, tok_rows, 3, HEADS * DH), new_accum[None])


def solution(mesh):
    in_specs = (
        P("section", "seq", None, None),
        P("section", "seq", None),
        P("section", None, None, "seq", None),
        P("section", None, None, "seq", None),
        P("section"),
        P("section"),
    )
    out_specs = (P("section", "seq", None, None), P("section", None, None, "seq", None))
    return jax.shard_map(
        per_device, mesh=mesh, in_specs=in_specs, out_specs=out_specs, check_vma=False
    )
```

profile of v0, /device:TPU:56, one launch (start us, length us, event | category | flops | bytes accessed | tf_op | source)
XLA Modules:
  0.0 327.7 jit_solution(9047187464734884413)
XLA Ops:
  3.1 11.6 %all-to-all-start.1 = ((bf16[32,1,64,128]{3,0,1,2:T(8,128)(2,1)}), bf16[32,1,64,128]{3,0,1,2:T(8,128)(2,1)S(1)}, u32[]{:S(2)}, u32[]{:S(2)}) async-start(bf16[32,1,64,128]{3,0,1,2:T(8,128)(2,1)} %copy.52), calls=%async_computation.1 | async-start | bytes 1048576 | tf_op jit(solution)/shard_map/all_to_all | solution.py:28
  17.3 14.1 %all-to-all-done.1 = bf16[32,1,64,128]{3,0,1,2:T(8,128)(2,1)S(1)} async-done(((bf16[32,1,64,128]{3,0,1,2:T(8,128)(2,1)}), bf16[32,1,64,128]{3,0,1,2:T(8,128)(2,1)S(1)}, u32[]{:S(2)}, u32[]{:S(2)}) %all-to-all-start.1) | async-done | bytes 524320 | tf_op jit(solution)/shard_map/all_to_all | solution.py:28
  32.2 6.9 %all-to-all-start = ((bf16[32,3,64,128]{3,0,1,2:T(8,128)(2,1)}), bf16[32,3,64,128]{3,0,1,2:T(8,128)(2,1)}, u32[]{:S(2)}, u32[]{:S(2)}) async-start(bf16[32,3,64,128]{3,0,1,2:T(8,128)(2,1)} %copy.49), calls=%async_computation | async-start | bytes 3145728 | tf_op jit(solution)/shard_map/all_to_all | solution.py:27
  39.1 2.7 copy.66
  47.9 30.2 %all-to-all-done = bf16[32,3,64,128]{3,0,1,2:T(8,128)(2,1)} async-done(((bf16[32,3,64,128]{3,0,1,2:T(8,128)(2,1)}), bf16[32,3,64,128]{3,0,1,2:T(8,128)(2,1)}, u32[]{:S(2)}, u32[]{:S(2)}) %all-to-all-start) | async-done | bytes 1572896 | tf_op jit(solution)/shard_map/all_to_all | solution.py:27
  82.5 130.7 %while.16 = (s32[]{:T(128)}, f32[5120,1,128]{0,2,1:T(8,128)S(1)}, f32[5120,1,128]{0,2,1:T(8,128)}, bf16[4,512,1,128]{3,1,2,0:T(8,128)(2,1)}, bf16[4,512,1,128]{3...) while((s32[]{:T(128)}, f32[5120,1,128]{0,2,1:T(8,128)S(1)}, ...), condition=%wide.region_4.5_spmd.clone.clone, body=%wide.region_0.4_spmd.clone.clone.sunk | while | flops 3411304448 | bytes 200771376 | solution.py:94
  85.1 4.6 %fusion.62 = (f32[512]{0:T(512)S(1)}, f32[512,5120]{1,0:T(8,128)S(1)}) fusion(bf16[5120,1,128]{2,0,1:T(8,128)(2,1)} %get-tuple-element.356, bf16[4,512,1,128]{3,1,2,0:T(8,128)(2,1)} %get-tuple-element.352, s32[]{:T(128)} %get-tuple-element.335, pred[5120]{0:T(1024)(128)(4,1)S(1)} %get-tuple-element.316, s32[512]{0:T(512)S(1)} %iota_add_fusion.4, ...), kind=kOutput, calls=%fused_computation.57.clone.1 | convolution fusion | flops 686816768 | bytes 11968000 | tf_op jit(solution)/shard_map/while/body/eval_jaxpr/qhd,khd->hqk/dot_general | solution.py:50
  89.7 4.0 %copy-done = f32[512,5120]{1,0:T(8,128)} copy-done((f32[512,5120]{1,0:T(8,128)}, f32[512,5120]{1,0:T(8,128)S(1)}, u32[]{:S(2)}) %copy-start) | copy-done | bytes 10485784 | tf_op jit(solution)/shard_map/while
  95.3 7.9 %fusion.65 = f32[5120,1,128]{0,2,1:T(8,128)} fusion(f32[5120,1,128]{0,2,1:T(8,128)} %get-tuple-element.337, pred[]{:T(512)S(6)} %compare.3, bf16[4,512,1,128]{3,1,2,0:T(8,128)(2,1)S(1)} %copy-done.9, s32[]{:T(128)} %get-tuple-element.335, f32[512,5120]{1,0:T(8,128)} %copy-done, f32[512]{0:T(512)S(1)} %fusion.63, f32[512]{0:T(512)S(1)} %get-tuple-element.319), kind=kOutput, calls=%fused_computation.11.clone.1 | convolution fusion | flops 680263680 | bytes 15863813 | tf_op jit(solution)/shard_map/while/body/eval_jaxpr/hqk,qhd->khd/dot_general | solution.py:75
  103.2 3.1 multiply_reduce_fusion.2
  106.3 3.6 %multiply_convert_fusion.2 = bf16[512,5120]{1,0:T(8,128)(2,1)S(1)} fusion(f32[512,5120]{1,0:T(8,128)S(1)} %get-tuple-element.320, f32[512]{0:T(512)S(1)} %get-tuple-element.321, f32[512]{0:T(512)S(1)} %fusion.63, f32[512,5120]{1,0:T(8,128)S(1)} %copy-done.1, f32[512]{0:T(512)S(1)} %get-tuple-element.319), kind=kLoop, calls=%fused_computation.2.clone.1 | loop fusion | flops 13107200 | bytes 26220544 | tf_op jit(solution)/shard_map/while/body/eval_jaxpr/convert_element_type | solution.py:65
  110.0 2.4 fusion.64
  117.2 4.6 %fusion.62 = (f32[512]{0:T(512)S(1)}, f32[512,5120]{1,0:T(8,128)S(1)}) fusion(bf16[5120,1,128]{2,0,1:T(8,128)(2,1)} %get-tuple-element.356, bf16[4,512,1,128]{3,1,2,0:T(8,128)(2,1)} %get-tuple-element.352, s32[]{:T(128)} %get-tuple-element.335, pred[5120]{0:T(1024)(128)(4,1)S(1)} %get-tuple-element.316, s32[512]{0:T(512)S(1)} %iota_add_fusion.4, ...), kind=kOutput, calls=%fused_computation.57.clone.1 | convolution fusion | flops 686816768 | bytes 11968000 | tf_op jit(solution)/shard_map/while/body/eval_jaxpr/qhd,khd->hqk/dot_general | solution.py:50
  121.8 4.0 %copy-done = f32[512,5120]{1,0:T(8,128)} copy-done((f32[512,5120]{1,0:T(8,128)}, f32[512,5120]{1,0:T(8,128)S(1)}, u32[]{:S(2)}) %copy-start) | copy-done | bytes 10485784 | tf_op jit(solution)/shard_map/while
  127.4 8.7 %fusion.65 = f32[5120,1,128]{0,2,1:T(8,128)} fusion(f32[5120,1,128]{0,2,1:T(8,128)} %get-tuple-element.337, pred[]{:T(512)S(6)} %compare.3, bf16[4,512,1,128]{3,1,2,0:T(8,128)(2,1)S(1)} %copy-done.9, s32[]{:T(128)} %get-tuple-element.335, f32[512,5120]{1,0:T(8,128)} %copy-done, f32[512]{0:T(512)S(1)} %fusion.63, f32[512]{0:T(512)S(1)} %get-tuple-element.319), kind=kOutput, calls=%fused_computation.11.clone.1 | convolution fusion | flops 680263680 | bytes 15863813 | tf_op jit(solution)/shard_map/while/body/eval_jaxpr/hqk,qhd->khd/dot_general | solution.py:75
  136.0 3.1 multiply_reduce_fusion.2
  139.2 3.6 %multiply_convert_fusion.2 = bf16[512,5120]{1,0:T(8,128)(2,1)S(1)} fusion(f32[512,5120]{1,0:T(8,128)S(1)} %get-tuple-element.320, f32[512]{0:T(512)S(1)} %get-tuple-element.321, f32[512]{0:T(512)S(1)} %fusion.63, f32[512,5120]{1,0:T(8,128)S(1)} %copy-done.1, f32[512]{0:T(512)S(1)} %get-tuple-element.319), kind=kLoop, calls=%fused_computation.2.clone.1 | loop fusion | flops 13107200 | bytes 26220544 | tf_op jit(solution)/shard_map/while/body/eval_jaxpr/convert_element_type | solution.py:65
  142.8 2.4 fusion.64
  150.1 4.6 %fusion.62 = (f32[512]{0:T(512)S(1)}, f32[512,5120]{1,0:T(8,128)S(1)}) fusion(bf16[5120,1,128]{2,0,1:T(8,128)(2,1)} %get-tuple-element.356, bf16[4,512,1,128]{3,1,2,0:T(8,128)(2,1)} %get-tuple-element.352, s32[]{:T(128)} %get-tuple-element.335, pred[5120]{0:T(1024)(128)(4,1)S(1)} %get-tuple-element.316, s32[512]{0:T(512)S(1)} %iota_add_fusion.4, ...), kind=kOutput, calls=%fused_computation.57.clone.1 | convolution fusion | flops 686816768 | bytes 11968000 | tf_op jit(solution)/shard_map/while/body/eval_jaxpr/qhd,khd->hqk/dot_general | solution.py:50
  154.7 4.0 %copy-done = f32[512,5120]{1,0:T(8,128)} copy-done((f32[512,5120]{1,0:T(8,128)}, f32[512,5120]{1,0:T(8,128)S(1)}, u32[]{:S(2)}) %copy-start) | copy-done | bytes 10485784 | tf_op jit(solution)/shard_map/while
  160.2 8.7 %fusion.65 = f32[5120,1,128]{0,2,1:T(8,128)} fusion(f32[5120,1,128]{0,2,1:T(8,128)} %get-tuple-element.337, pred[]{:T(512)S(6)} %compare.3, bf16[4,512,1,128]{3,1,2,0:T(8,128)(2,1)S(1)} %copy-done.9, s32[]{:T(128)} %get-tuple-element.335, f32[512,5120]{1,0:T(8,128)} %copy-done, f32[512]{0:T(512)S(1)} %fusion.63, f32[512]{0:T(512)S(1)} %get-tuple-element.319), kind=kOutput, calls=%fused_computation.11.clone.1 | convolution fusion | flops 680263680 | bytes 15863813 | tf_op jit(solution)/shard_map/while/body/eval_jaxpr/hqk,qhd->khd/dot_general | solution.py:75
  168.9 3.1 multiply_reduce_fusion.2
  172.0 3.6 %multiply_convert_fusion.2 = bf16[512,5120]{1,0:T(8,128)(2,1)S(1)} fusion(f32[512,5120]{1,0:T(8,128)S(1)} %get-tuple-element.320, f32[512]{0:T(512)S(1)} %get-tuple-element.321, f32[512]{0:T(512)S(1)} %fusion.63, f32[512,5120]{1,0:T(8,128)S(1)} %copy-done.1, f32[512]{0:T(512)S(1)} %get-tuple-element.319), kind=kLoop, calls=%fused_computation.2.clone.1 | loop fusion | flops 13107200 | bytes 26220544 | tf_op jit(solution)/shard_map/while/body/eval_jaxpr/convert_element_type | solution.py:65
  182.9 4.6 %fusion.62 = (f32[512]{0:T(512)S(1)}, f32[512,5120]{1,0:T(8,128)S(1)}) fusion(bf16[5120,1,128]{2,0,1:T(8,128)(2,1)} %get-tuple-element.356, bf16[4,512,1,128]{3,1,2,0:T(8,128)(2,1)} %get-tuple-element.352, s32[]{:T(128)} %get-tuple-element.335, pred[5120]{0:T(1024)(128)(4,1)S(1)} %get-tuple-element.316, s32[512]{0:T(512)S(1)} %iota_add_fusion.4, ...), kind=kOutput, calls=%fused_computation.57.clone.1 | convolution fusion | flops 686816768 | bytes 11968000 | tf_op jit(solution)/shard_map/while/body/eval_jaxpr/qhd,khd->hqk/dot_general | solution.py:50
  187.5 4.0 %copy-done = f32[512,5120]{1,0:T(8,128)} copy-done((f32[512,5120]{1,0:T(8,128)}, f32[512,5120]{1,0:T(8,128)S(1)}, u32[]{:S(2)}) %copy-start) | copy-done | bytes 10485784 | tf_op jit(solution)/shard_map/while
  193.1 8.7 %fusion.65 = f32[5120,1,128]{0,2,1:T(8,128)} fusion(f32[5120,1,128]{0,2,1:T(8,128)} %get-tuple-element.337, pred[]{:T(512)S(6)} %compare.3, bf16[4,512,1,128]{3,1,2,0:T(8,128)(2,1)S(1)} %copy-done.9, s32[]{:T(128)} %get-tuple-element.335, f32[512,5120]{1,0:T(8,128)} %copy-done, f32[512]{0:T(512)S(1)} %fusion.63, f32[512]{0:T(512)S(1)} %get-tuple-element.319), kind=kOutput, calls=%fused_computation.11.clone.1 | convolution fusion | flops 680263680 | bytes 15863813 | tf_op jit(solution)/shard_map/while/body/eval_jaxpr/hqk,qhd->khd/dot_general | solution.py:75
  201.8 3.1 multiply_reduce_fusion.2
  204.9 3.6 %multiply_convert_fusion.2 = bf16[512,5120]{1,0:T(8,128)(2,1)S(1)} fusion(f32[512,5120]{1,0:T(8,128)S(1)} %get-tuple-element.320, f32[512]{0:T(512)S(1)} %get-tuple-element.321, f32[512]{0:T(512)S(1)} %fusion.63, f32[512,5120]{1,0:T(8,128)S(1)} %copy-done.1, f32[512]{0:T(512)S(1)} %get-tuple-element.319), kind=kLoop, calls=%fused_computation.2.clone.1 | loop fusion | flops 13107200 | bytes 26220544 | tf_op jit(solution)/shard_map/while/body/eval_jaxpr/convert_element_type | solution.py:65
  220.8 10.0 %copy.58 = bf16[2048,3,1,128]{3,1,2,0:T(4,128)(2,1)S(1)} copy(bf16[2048,3,1,128]{3,0,2,1:T(8,128)(2,1)S(1)} %pad_maximum_fusion) | data formatting | bytes 3145728 | tf_op jit(solution)/shard_map/stack | solution.py:98
  230.8 56.5 %all_to_all.51 = bf16[2048,3,1,128]{3,1,2,0:T(4,128)(2,1)S(1)} all-to-all(bf16[2048,3,1,128]{3,1,2,0:T(4,128)(2,1)S(1)} %copy.58), channel_id=1, replica_groups=mesh['section'=4,'seq'=64] {'seq'}, dimensions={0} | all-to-all | bytes 3145728 | tf_op jit(solution)/shard_map/all_to_all | solution.py:106
  289.9 5.0 %maximum_add_fusion = f32[1,3072,2,1,128]{4,3,2,1,0:T(1,128)} fusion(f32[1,3072,2,1,128]{4,3,2,1,0:T(1,128)S(1)} %copy-done.3, f32[1,3072,1,1,128]{4,3,2,1,0:T(1,128)S(1)} %bitcast.146, f32[1,3072,1,1,128]{4,3,2,1,0:T(1,128)S(1)} %bitcast.143), kind=kLoop, calls=%fused_computation.40 | loop fusion | flops 1572864 | bytes 9437184 | tf_op jit(solution)/shard_map/add | solution.py:97
  294.9 30.1 %collective-permute-done = bf16[32,3,64,128]{3,0,2,1:T(8,128)(2,1)S(1)} collective-permute-done((bf16[32,3,64,128]{3,0,2,1:T(8,128)(2,1)S(1)}, bf16[32,3,64,128]{3,0,2,1:T(8,128)(2,1)S(1)}, u32[]{:S(2)}, u32[]{:S(2)}) %collective-permute-start) | collective-permute-done | bytes 1572896 | tf_op jit(solution)/shard_map/ppermute | solution.py:14
  (102 shorter events, 58.8 us)
Async XLA Ops:
  0.6 14.0 %copy-start.6 = (bf16[1,32,3,8192]{3,1,2,0:T(8,128)(2,1)S(1)}, bf16[1,32,3,8192]{3,1,2,0:T(8,128)(2,1)}, u32[]{:S(2)}) copy-start(bf16[1,32,3,8192]{3,1,2,0:T(8,128)(2,1)} %param.8) | copy-start | bytes 4718596
  3.1 28.3 %all-to-all-start.1 = ((bf16[32,1,64,128]{3,0,1,2:T(8,128)(2,1)}), bf16[32,1,64,128]{3,0,1,2:T(8,128)(2,1)S(1)}, u32[]{:S(2)}, u32[]{:S(2)}) async-start(bf16[32,1,64,128]{3,0,1,2:T(8,128)(2,1)} %copy.52), calls=%async_computation.1 | async-start | bytes 1048576 | tf_op jit(solution)/shard_map/all_to_all | solution.py:28
  31.3 0.8 copy-start.4
  32.2 46.0 %all-to-all-start = ((bf16[32,3,64,128]{3,0,1,2:T(8,128)(2,1)}), bf16[32,3,64,128]{3,0,1,2:T(8,128)(2,1)}, u32[]{:S(2)}, u32[]{:S(2)}) async-start(bf16[32,3,64,128]{3,0,1,2:T(8,128)(2,1)} %copy.49), calls=%async_computation | async-start | bytes 3145728 | tf_op jit(solution)/shard_map/all_to_all | solution.py:27
  78.1 2.7 copy-start.2
  89.7 4.0 %copy-start = (f32[512,5120]{1,0:T(8,128)}, f32[512,5120]{1,0:T(8,128)S(1)}, u32[]{:S(2)}) copy-start(f32[512,5120]{1,0:T(8,128)S(1)} %get-tuple-element.318) | copy-start | bytes 31457284 | tf_op jit(solution)/shard_map/while
  93.7 1.6 copy-start.9
  95.2 7.9 %copy-start.1 = (f32[512,5120]{1,0:T(8,128)S(1)}, f32[512,5120]{1,0:T(8,128)}, u32[]{:S(2)}) copy-start(f32[512,5120]{1,0:T(8,128)} %copy-done) | copy-start | bytes 31457284 | tf_op jit(solution)/shard_map/while
  95.3 7.9 %copy-start.8 = (bf16[5120,1,128]{2,0,1:T(8,128)(2,1)S(1)}, bf16[5120,1,128]{2,0,1:T(8,128)(2,1)}, u32[]{:S(2)}) copy-start(bf16[5120,1,128]{2,0,1:T(8,128)(2,1)} %get-tuple-element.358) | copy-start | bytes 3932164 | tf_op jit(solution)/shard_map/while
  109.9 2.5 copy-start.7
  121.8 4.0 %copy-start = (f32[512,5120]{1,0:T(8,128)}, f32[512,5120]{1,0:T(8,128)S(1)}, u32[]{:S(2)}) copy-start(f32[512,5120]{1,0:T(8,128)S(1)} %get-tuple-element.318) | copy-start | bytes 31457284 | tf_op jit(solution)/shard_map/while
  125.8 1.6 copy-start.9
  127.4 8.7 %copy-start.1 = (f32[512,5120]{1,0:T(8,128)S(1)}, f32[512,5120]{1,0:T(8,128)}, u32[]{:S(2)}) copy-start(f32[512,5120]{1,0:T(8,128)} %copy-done) | copy-start | bytes 31457284 | tf_op jit(solution)/shard_map/while
  127.4 8.7 %copy-start.8 = (bf16[5120,1,128]{2,0,1:T(8,128)(2,1)S(1)}, bf16[5120,1,128]{2,0,1:T(8,128)(2,1)}, u32[]{:S(2)}) copy-start(bf16[5120,1,128]{2,0,1:T(8,128)(2,1)} %get-tuple-element.358) | copy-start | bytes 3932164 | tf_op jit(solution)/shard_map/while
  142.8 2.5 copy-start.7
  154.6 4.0 %copy-start = (f32[512,5120]{1,0:T(8,128)}, f32[512,5120]{1,0:T(8,128)S(1)}, u32[]{:S(2)}) copy-start(f32[512,5120]{1,0:T(8,128)S(1)} %get-tuple-element.318) | copy-start | bytes 31457284 | tf_op jit(solution)/shard_map/while
  158.6 1.6 copy-start.9
  160.2 8.7 %copy-start.1 = (f32[512,5120]{1,0:T(8,128)S(1)}, f32[512,5120]{1,0:T(8,128)}, u32[]{:S(2)}) copy-start(f32[512,5120]{1,0:T(8,128)} %copy-done) | copy-start | bytes 31457284 | tf_op jit(solution)/shard_map/while
  160.2 8.7 %copy-start.8 = (bf16[5120,1,128]{2,0,1:T(8,128)(2,1)S(1)}, bf16[5120,1,128]{2,0,1:T(8,128)(2,1)}, u32[]{:S(2)}) copy-start(bf16[5120,1,128]{2,0,1:T(8,128)(2,1)} %get-tuple-element.358) | copy-start | bytes 3932164 | tf_op jit(solution)/shard_map/while
  175.7 2.5 copy-start.7
  187.5 4.0 %copy-start = (f32[512,5120]{1,0:T(8,128)}, f32[512,5120]{1,0:T(8,128)S(1)}, u32[]{:S(2)}) copy-start(f32[512,5120]{1,0:T(8,128)S(1)} %get-tuple-element.318) | copy-start | bytes 31457284 | tf_op jit(solution)/shard_map/while
  191.5 1.6 copy-start.9
  193.1 8.7 %copy-start.1 = (f32[512,5120]{1,0:T(8,128)S(1)}, f32[512,5120]{1,0:T(8,128)}, u32[]{:S(2)}) copy-start(f32[512,5120]{1,0:T(8,128)} %copy-done) | copy-start | bytes 31457284 | tf_op jit(solution)/shard_map/while
  193.1 8.7 %copy-start.8 = (bf16[5120,1,128]{2,0,1:T(8,128)(2,1)S(1)}, bf16[5120,1,128]{2,0,1:T(8,128)(2,1)}, u32[]{:S(2)}) copy-start(bf16[5120,1,128]{2,0,1:T(8,128)(2,1)} %get-tuple-element.358) | copy-start | bytes 3932164 | tf_op jit(solution)/shard_map/while
  208.5 2.5 copy-start.7
  217.3 2.3 copy-start.5
  287.5 1.4 slice-start
  287.5 2.4 copy-start.3
  287.5 37.5 %collective-permute-start = (bf16[32,3,64,128]{3,0,2,1:T(8,128)(2,1)S(1)}, bf16[32,3,64,128]{3,0,2,1:T(8,128)(2,1)S(1)}, u32[]{:S(2)}, u32[]{:S(2)}) collective-permute-start(bf16[32,3,64,128]{3,0,2,1:T(8,128)(2,1)S(1)} %bitcast.152), channel_id=1, source_target_pairs={{64,0},{128,64},{192,128},{0,192},{65,1},{129,65},{193,129},{1,193... | collective-permute-start | bytes 4718600 | tf_op jit(solution)/shard_map/ppermute | solution.py:14
where the time goes:
time: 329 us; the launch traced here: 328 us
  matrix products  83.2 us (25%)
  waiting for transfers between devices  74.4 us (23%)
  blocking collectives  56.5 us (17%)
  local copies, waits for them, and re-layouts  53.9 us (16%)
  other arithmetic  38.6 us (12%)
  starting transfers between devices  19.3 us (6%)
    all_to_all x1, blocking collectives, per_device(): lax.all_to_all(span_grads, 'seq', split_axis=0, concat_axis=2, tiled=True)  56.5 us
    dot_general x4, matrix products, backward_block(): jnp.einsum('hqk,qhd->khd', attention_low, dout_block, preferred_element_t...  33.9 us
    all_to_all x1, waiting for transfers between devices, per_device(): lax.all_to_all(local_rows, 'seq', split_axis=2, concat_axis=0, tiled=True)  30.2 us
    ppermute x1, waiting for transfers between devices, from_behind(): return lax.ppermute(block, axis, route)  30.1 us
    dot_general x4, matrix products, scores(): jnp.einsum('qhd,khd->hqk', query_block, all_keys, preferred_element_type=...  18.3 us
    while x40, local copies, waits for them, and re-layouts  16 us
    convert_element_type x4, other arithmetic, backward_block(): dscores = (attention * (dprobs - row_delta)).astype(jnp.bfloat16)  14.5 us
    all_to_all x1, waiting for transfers between devices, per_device(): lax.all_to_all(upstream, 'seq', split_axis=2, concat_axis=0, tiled=True)  14.1 us
  transfers between devices with their start and end apart: 3, of which 3 were waited for; matrix products, arithmetic and copies ran while one was open for 5% of the time, Pallas kernels for 0%

commit v1 on v0

--- a/solution.py
+++ b/solution.py
@@ -103,7 +103,11 @@
         ],
         axis=1,
     )
-    regrouped = lax.all_to_all(span_grads, "seq", split_axis=0, concat_axis=2, tiled=True)
+    next_value = lax.psum(1, axis_name="seq")
+    current_value = jnp.split(span_grads, next_value, axis=0)
+    part_next = jnp.stack(current_value, axis=0)
+    arr_out = lax.all_to_all(part_next, axis_name="seq", split_axis=0, concat_axis=0)
+    regrouped = jnp.concatenate(arr_out, axis=2)
     moved = from_behind(regrouped, "section", -1)
     return (moved.reshape(1, tok_rows, 3, HEADS * DH), new_accum[None])
 

time: 329 us -> 309 us (0.939)
  blocking collectives: 56.5 us -> 45.2 us
  local copies, waits for them, and re-layouts: 53.9 us -> 45.7 us
    all_to_all x1, blocking collectives: 56.5 us -> 45.2 us  [per_device(): lax.all_to_all(part_next, axis_name='seq', split_axis=0, concat_axis=0)]
    another operation x3 -> x2, local copies, waits for them, and re-layouts: 12.1 us -> 2.12 us  [per_device(): jnp.stack([grad_query.reshape(span_len, local_heads, DH), grad_keys[past_...]
    unnamed x14 -> x79, local copies, waits for them, and re-layouts: 7.13 us -> 8.91 us
where the time goes in v1:
time: 309 us; the launch traced here: 308 us
  matrix products  83.2 us (27%)
  waiting for transfers between devices  74.7 us (24%)
  local copies, waits for them, and re-layouts  45.7 us (15%)
  blocking collectives  45.2 us (15%)
  other arithmetic  37.7 us (12%)
  starting transfers between devices  19.3 us (6%)
    all_to_all x1, blocking collectives, per_device(): lax.all_to_all(part_next, axis_name='seq', split_axis=0, concat_axis=0)  45.2 us
    dot_general x4, matrix products, backward_block(): jnp.einsum('hqk,qhd->khd', attention_low, dout_block, preferred_element_t...  33.9 us
    all_to_all x1, waiting for transfers between devices, per_device(): lax.all_to_all(local_rows, 'seq', split_axis=2, concat_axis=0, tiled=True)  31.2 us
    ppermute x1, waiting for transfers between devices, from_behind(): return lax.ppermute(block, axis, route)  29.5 us
    dot_general x4, matrix products, scores(): jnp.einsum('qhd,khd->hqk', query_block, all_keys, preferred_element_type=...  18.3 us
    while x40, local copies, waits for them, and re-layouts  16 us
    convert_element_type x4, other arithmetic, backward_block(): dscores = (attention * (dprobs - row_delta)).astype(jnp.bfloat16)  14.5 us
    all_to_all x1, waiting for transfers between devices, per_device(): lax.all_to_all(upstream, 'seq', split_axis=2, concat_axis=0, tiled=True)  14.1 us
  transfers between devices with their start and end apart: 3, of which 3 were waited for; matrix products, arithmetic and copies ran while one was open for 5% of the time, Pallas kernels for 0%

profile of v1, /device:TPU:56, one launch (start us, length us, event | category | flops | bytes accessed | tf_op | source)
XLA Modules:
  0.0 307.8 jit_solution(17523351807792778259)
XLA Ops:
  3.1 11.6 %all-to-all-start.1 = ((bf16[32,1,64,128]{3,0,1,2:T(8,128)(2,1)}), bf16[32,1,64,128]{3,0,1,2:T(8,128)(2,1)S(1)}, u32[]{:S(2)}, u32[]{:S(2)}) async-start(bf16[32,1,64,128]{3,0,1,2:T(8,128)(2,1)} %copy.303), calls=%async_computation.1 | async-start | bytes 1048576 | tf_op jit(solution)/shard_map/all_to_all | solution.py:28
  17.3 14.1 %all-to-all-done.1 = bf16[32,1,64,128]{3,0,1,2:T(8,128)(2,1)S(1)} async-done(((bf16[32,1,64,128]{3,0,1,2:T(8,128)(2,1)}), bf16[32,1,64,128]{3,0,1,2:T(8,128)(2,1)S(1)}, u32[]{:S(2)}, u32[]{:S(2)}) %all-to-all-start.1) | async-done | bytes 524320 | tf_op jit(solution)/shard_map/all_to_all | solution.py:28
  32.1 6.9 %all-to-all-start = ((bf16[32,3,64,128]{3,0,1,2:T(8,128)(2,1)}), bf16[32,3,64,128]{3,0,1,2:T(8,128)(2,1)}, u32[]{:S(2)}, u32[]{:S(2)}) async-start(bf16[32,3,64,128]{3,0,1,2:T(8,128)(2,1)} %copy.300), calls=%async_computation | async-start | bytes 3145728 | tf_op jit(solution)/shard_map/all_to_all | solution.py:27
  39.0 2.8 copy.379
  46.9 31.2 %all-to-all-done = bf16[32,3,64,128]{3,0,1,2:T(8,128)(2,1)} async-done(((bf16[32,3,64,128]{3,0,1,2:T(8,128)(2,1)}), bf16[32,3,64,128]{3,0,1,2:T(8,128)(2,1)}, u32[]{:S(2)}, u32[]{:S(2)}) %all-to-all-start) | async-done | bytes 1572896 | tf_op jit(solution)/shard_map/all_to_all | solution.py:27
  82.8 130.6 %while.16 = (s32[]{:T(128)}, f32[5120,1,128]{0,2,1:T(8,128)S(1)}, f32[5120,1,128]{0,2,1:T(8,128)}, bf16[4,512,1,128]{3,1,2,0:T(8,128)(2,1)}, bf16[4,512,1,128]{3...) while((s32[]{:T(128)}, f32[5120,1,128]{0,2,1:T(8,128)S(1)}, ...), condition=%wide.region_4.5_spmd.clone.clone, body=%wide.region_0.4_spmd.clone.clone.sunk | while | flops 3411304448 | bytes 200771376 | solution.py:94
  85.3 4.6 %fusion.62 = (f32[512]{0:T(512)S(1)}, f32[512,5120]{1,0:T(8,128)S(1)}) fusion(bf16[5120,1,128]{2,0,1:T(8,128)(2,1)} %get-tuple-element.358, bf16[4,512,1,128]{3,1,2,0:T(8,128)(2,1)} %get-tuple-element.354, s32[]{:T(128)} %get-tuple-element.337, pred[5120]{0:T(1024)(128)(4,1)S(1)} %get-tuple-element.318, s32[512]{0:T(512)S(1)} %iota_add_fusion.4, ...), kind=kOutput, calls=%fused_computation.185.clone.1 | convolution fusion | flops 686816768 | bytes 11968000 | tf_op jit(solution)/shard_map/while/body/eval_jaxpr/qhd,khd->hqk/dot_general | solution.py:50
  89.9 4.0 %copy-done = f32[512,5120]{1,0:T(8,128)} copy-done((f32[512,5120]{1,0:T(8,128)}, f32[512,5120]{1,0:T(8,128)S(1)}, u32[]{:S(2)}) %copy-start) | copy-done | bytes 10485784 | tf_op jit(solution)/shard_map/while
  95.5 7.9 %fusion.65 = f32[5120,1,128]{0,2,1:T(8,128)} fusion(f32[5120,1,128]{0,2,1:T(8,128)} %get-tuple-element.339, pred[]{:T(512)S(6)} %compare.3, bf16[4,512,1,128]{3,1,2,0:T(8,128)(2,1)S(1)} %copy-done.10, s32[]{:T(128)} %get-tuple-element.337, f32[512,5120]{1,0:T(8,128)} %copy-done, f32[512]{0:T(512)S(1)} %fusion.63, f32[512]{0:T(512)S(1)} %get-tuple-element.321), kind=kOutput, calls=%fused_computation.11.clone.1 | convolution fusion | flops 680263680 | bytes 15863813 | tf_op jit(solution)/shard_map/while/body/eval_jaxpr/hqk,qhd->khd/dot_general | solution.py:75
  103.4 3.1 %multiply_reduce_fusion.2 = (f32[512]{0:T(512)S(1)}, f32[512,5120]{1,0:T(8,128)S(1)}) fusion(f32[512]{0:T(512)S(1)} %fusion.63, f32[512,5120]{1,0:T(8,128)S(1)} %copy-done.1, f32[512]{0:T(512)S(1)} %get-tuple-element.321, bf16[5120,1,128]{2,0,1:T(8,128)(2,1)S(1)} %copy-done.9, bf16[4,512,1,128]{3,1,2,0:T(8,128)(2,1)S(1)} %copy-done.10, ...), kind=kOutput, calls=%fused_computation.3.clone.1 | convolution fusion | flops 681573888 | bytes 22419460 | tf_op jit(solution)/shard_map/while/body/eval_jaxpr/qhd,khd->hqk/dot_general | solution.py:61
  106.6 3.6 %multiply_convert_fusion.2 = bf16[512,5120]{1,0:T(8,128)(2,1)S(1)} fusion(f32[512,5120]{1,0:T(8,128)S(1)} %get-tuple-element.322, f32[512]{0:T(512)S(1)} %get-tuple-element.323, f32[512]{0:T(512)S(1)} %fusion.63, f32[512,5120]{1,0:T(8,128)S(1)} %copy-done.1, f32[512]{0:T(512)S(1)} %get-tuple-element.321), kind=kLoop, calls=%fused_computation.2.clone.1 | loop fusion | flops 13107200 | bytes 26220544 | tf_op jit(solution)/shard_map/while/body/eval_jaxpr/convert_element_type | solution.py:65
  117.4 4.6 %fusion.62 = (f32[512]{0:T(512)S(1)}, f32[512,5120]{1,0:T(8,128)S(1)}) fusion(bf16[5120,1,128]{2,0,1:T(8,128)(2,1)} %get-tuple-element.358, bf16[4,512,1,128]{3,1,2,0:T(8,128)(2,1)} %get-tuple-element.354, s32[]{:T(128)} %get-tuple-element.337, pred[5120]{0:T(1024)(128)(4,1)S(1)} %get-tuple-element.318, s32[512]{0:T(512)S(1)} %iota_add_fusion.4, ...), kind=kOutput, calls=%fused_computation.185.clone.1 | convolution fusion | flops 686816768 | bytes 11968000 | tf_op jit(solution)/shard_map/while/body/eval_jaxpr/qhd,khd->hqk/dot_general | solution.py:50
  122.0 4.0 %copy-done = f32[512,5120]{1,0:T(8,128)} copy-done((f32[512,5120]{1,0:T(8,128)}, f32[512,5120]{1,0:T(8,128)S(1)}, u32[]{:S(2)}) %copy-start) | copy-done | bytes 10485784 | tf_op jit(solution)/shard_map/while
  127.6 8.7 %fusion.65 = f32[5120,1,128]{0,2,1:T(8,128)} fusion(f32[5120,1,128]{0,2,1:T(8,128)} %get-tuple-element.339, pred[]{:T(512)S(6)} %compare.3, bf16[4,512,1,128]{3,1,2,0:T(8,128)(2,1)S(1)} %copy-done.10, s32[]{:T(128)} %get-tuple-element.337, f32[512,5120]{1,0:T(8,128)} %copy-done, f32[512]{0:T(512)S(1)} %fusion.63, f32[512]{0:T(512)S(1)} %get-tuple-element.321), kind=kOutput, calls=%fused_computation.11.clone.1 | convolution fusion | flops 680263680 | bytes 15863813 | tf_op jit(solution)/shard_map/while/body/eval_jaxpr/hqk,qhd->khd/dot_general | solution.py:75
  136.3 3.1 %multiply_reduce_fusion.2 = (f32[512]{0:T(512)S(1)}, f32[512,5120]{1,0:T(8,128)S(1)}) fusion(f32[512]{0:T(512)S(1)} %fusion.63, f32[512,5120]{1,0:T(8,128)S(1)} %copy-done.1, f32[512]{0:T(512)S(1)} %get-tuple-element.321, bf16[5120,1,128]{2,0,1:T(8,128)(2,1)S(1)} %copy-done.9, bf16[4,512,1,128]{3,1,2,0:T(8,128)(2,1)S(1)} %copy-done.10, ...), kind=kOutput, calls=%fused_computation.3.clone.1 | convolution fusion | flops 681573888 | bytes 22419460 | tf_op jit(solution)/shard_map/while/body/eval_jaxpr/qhd,khd->hqk/dot_general | solution.py:61
  139.4 3.6 %multiply_convert_fusion.2 = bf16[512,5120]{1,0:T(8,128)(2,1)S(1)} fusion(f32[512,5120]{1,0:T(8,128)S(1)} %get-tuple-element.322, f32[512]{0:T(512)S(1)} %get-tuple-element.323, f32[512]{0:T(512)S(1)} %fusion.63, f32[512,5120]{1,0:T(8,128)S(1)} %copy-done.1, f32[512]{0:T(512)S(1)} %get-tuple-element.321), kind=kLoop, calls=%fused_computation.2.clone.1 | loop fusion | flops 13107200 | bytes 26220544 | tf_op jit(solution)/shard_map/while/body/eval_jaxpr/convert_element_type | solution.py:65
  143.0 2.4 fusion.64
  150.2 4.6 %fusion.62 = (f32[512]{0:T(512)S(1)}, f32[512,5120]{1,0:T(8,128)S(1)}) fusion(bf16[5120,1,128]{2,0,1:T(8,128)(2,1)} %get-tuple-element.358, bf16[4,512,1,128]{3,1,2,0:T(8,128)(2,1)} %get-tuple-element.354, s32[]{:T(128)} %get-tuple-element.337, pred[5120]{0:T(1024)(128)(4,1)S(1)} %get-tuple-element.318, s32[512]{0:T(512)S(1)} %iota_add_fusion.4, ...), kind=kOutput, calls=%fused_computation.185.clone.1 | convolution fusion | flops 686816768 | bytes 11968000 | tf_op jit(solution)/shard_map/while/body/eval_jaxpr/qhd,khd->hqk/dot_general | solution.py:50
  154.8 4.0 %copy-done = f32[512,5120]{1,0:T(8,128)} copy-done((f32[512,5120]{1,0:T(8,128)}, f32[512,5120]{1,0:T(8,128)S(1)}, u32[]{:S(2)}) %copy-start) | copy-done | bytes 10485784 | tf_op jit(solution)/shard_map/while
  160.4 8.7 %fusion.65 = f32[5120,1,128]{0,2,1:T(8,128)} fusion(f32[5120,1,128]{0,2,1:T(8,128)} %get-tuple-element.339, pred[]{:T(512)S(6)} %compare.3, bf16[4,512,1,128]{3,1,2,0:T(8,128)(2,1)S(1)} %copy-done.10, s32[]{:T(128)} %get-tuple-element.337, f32[512,5120]{1,0:T(8,128)} %copy-done, f32[512]{0:T(512)S(1)} %fusion.63, f32[512]{0:T(512)S(1)} %get-tuple-element.321), kind=kOutput, calls=%fused_computation.11.clone.1 | convolution fusion | flops 680263680 | bytes 15863813 | tf_op jit(solution)/shard_map/while/body/eval_jaxpr/hqk,qhd->khd/dot_general | solution.py:75
  169.1 3.1 %multiply_reduce_fusion.2 = (f32[512]{0:T(512)S(1)}, f32[512,5120]{1,0:T(8,128)S(1)}) fusion(f32[512]{0:T(512)S(1)} %fusion.63, f32[512,5120]{1,0:T(8,128)S(1)} %copy-done.1, f32[512]{0:T(512)S(1)} %get-tuple-element.321, bf16[5120,1,128]{2,0,1:T(8,128)(2,1)S(1)} %copy-done.9, bf16[4,512,1,128]{3,1,2,0:T(8,128)(2,1)S(1)} %copy-done.10, ...), kind=kOutput, calls=%fused_computation.3.clone.1 | convolution fusion | flops 681573888 | bytes 22419460 | tf_op jit(solution)/shard_map/while/body/eval_jaxpr/qhd,khd->hqk/dot_general | solution.py:61
  172.2 3.6 %multiply_convert_fusion.2 = bf16[512,5120]{1,0:T(8,128)(2,1)S(1)} fusion(f32[512,5120]{1,0:T(8,128)S(1)} %get-tuple-element.322, f32[512]{0:T(512)S(1)} %get-tuple-element.323, f32[512]{0:T(512)S(1)} %fusion.63, f32[512,5120]{1,0:T(8,128)S(1)} %copy-done.1, f32[512]{0:T(512)S(1)} %get-tuple-element.321), kind=kLoop, calls=%fused_computation.2.clone.1 | loop fusion | flops 13107200 | bytes 26220544 | tf_op jit(solution)/shard_map/while/body/eval_jaxpr/convert_element_type | solution.py:65
  175.8 2.4 fusion.64
  183.1 4.6 %fusion.62 = (f32[512]{0:T(512)S(1)}, f32[512,5120]{1,0:T(8,128)S(1)}) fusion(bf16[5120,1,128]{2,0,1:T(8,128)(2,1)} %get-tuple-element.358, bf16[4,512,1,128]{3,1,2,0:T(8,128)(2,1)} %get-tuple-element.354, s32[]{:T(128)} %get-tuple-element.337, pred[5120]{0:T(1024)(128)(4,1)S(1)} %get-tuple-element.318, s32[512]{0:T(512)S(1)} %iota_add_fusion.4, ...), kind=kOutput, calls=%fused_computation.185.clone.1 | convolution fusion | flops 686816768 | bytes 11968000 | tf_op jit(solution)/shard_map/while/body/eval_jaxpr/qhd,khd->hqk/dot_general | solution.py:50
  187.7 4.0 %copy-done = f32[512,5120]{1,0:T(8,128)} copy-done((f32[512,5120]{1,0:T(8,128)}, f32[512,5120]{1,0:T(8,128)S(1)}, u32[]{:S(2)}) %copy-start) | copy-done | bytes 10485784 | tf_op jit(solution)/shard_map/while
  193.3 8.7 %fusion.65 = f32[5120,1,128]{0,2,1:T(8,128)} fusion(f32[5120,1,128]{0,2,1:T(8,128)} %get-tuple-element.339, pred[]{:T(512)S(6)} %compare.3, bf16[4,512,1,128]{3,1,2,0:T(8,128)(2,1)S(1)} %copy-done.10, s32[]{:T(128)} %get-tuple-element.337, f32[512,5120]{1,0:T(8,128)} %copy-done, f32[512]{0:T(512)S(1)} %fusion.63, f32[512]{0:T(512)S(1)} %get-tuple-element.321), kind=kOutput, calls=%fused_computation.11.clone.1 | convolution fusion | flops 680263680 | bytes 15863813 | tf_op jit(solution)/shard_map/while/body/eval_jaxpr/hqk,qhd->khd/dot_general | solution.py:75
  201.9 3.1 %multiply_reduce_fusion.2 = (f32[512]{0:T(512)S(1)}, f32[512,5120]{1,0:T(8,128)S(1)}) fusion(f32[512]{0:T(512)S(1)} %fusion.63, f32[512,5120]{1,0:T(8,128)S(1)} %copy-done.1, f32[512]{0:T(512)S(1)} %get-tuple-element.321, bf16[5120,1,128]{2,0,1:T(8,128)(2,1)S(1)} %copy-done.9, bf16[4,512,1,128]{3,1,2,0:T(8,128)(2,1)S(1)} %copy-done.10, ...), kind=kOutput, calls=%fused_computation.3.clone.1 | convolution fusion | flops 681573888 | bytes 22419460 | tf_op jit(solution)/shard_map/while/body/eval_jaxpr/qhd,khd->hqk/dot_general | solution.py:61
  205.0 3.6 %multiply_convert_fusion.2 = bf16[512,5120]{1,0:T(8,128)(2,1)S(1)} fusion(f32[512,5120]{1,0:T(8,128)S(1)} %get-tuple-element.322, f32[512]{0:T(512)S(1)} %get-tuple-element.323, f32[512]{0:T(512)S(1)} %fusion.63, f32[512,5120]{1,0:T(8,128)S(1)} %copy-done.1, f32[512]{0:T(512)S(1)} %get-tuple-element.321), kind=kLoop, calls=%fused_computation.2.clone.1 | loop fusion | flops 13107200 | bytes 26220544 | tf_op jit(solution)/shard_map/while/body/eval_jaxpr/convert_element_type | solution.py:65
  208.7 2.4 fusion.64
  222.1 45.2 %all_to_all.38 = bf16[64,32,3,1,128]{4,1,3,2,0:T(8,128)(2,1)S(1)} all-to-all(bf16[64,32,3,1,128]{4,1,3,2,0:T(8,128)(2,1)S(1)} %constant_dynamic-update-slice_fusion), channel_id=1, replica_groups=mesh['section'=4,'seq'=64] {'seq'}, dimensions={0} | all-to-all | bytes 3145728 | tf_op jit(solution)/shard_map/all_to_all | solution.py:109
  271.1 5.0 %maximum_add_fusion = f32[1,3072,2,1,128]{4,3,2,1,0:T(1,128)} fusion(f32[1,3072,2,1,128]{4,3,2,1,0:T(1,128)S(1)} %copy-done.3, f32[1,3072,1,1,128]{4,3,2,1,0:T(1,128)S(1)} %bitcast.526, f32[1,3072,1,1,128]{4,3,2,1,0:T(1,128)S(1)} %bitcast.523), kind=kLoop, calls=%fused_computation.40 | loop fusion | flops 1572864 | bytes 9437184 | tf_op jit(solution)/shard_map/add | solution.py:97
  276.1 29.5 %collective-permute-done = bf16[32,3,64,128]{3,2,1,0:T(8,128)(2,1)S(1)} collective-permute-done((bf16[32,3,64,128]{3,2,1,0:T(8,128)(2,1)S(1)}, bf16[32,3,64,128]{3,2,1,0:T(8,128)(2,1)S(1)}, u32[]{:S(2)}, u32[]{:S(2)}) %collective-permute-start) | collective-permute-done | bytes 1572896 | tf_op jit(solution)/shard_map/ppermute | solution.py:14
  (167 shorter events, 57.1 us)
Async XLA Ops:
  0.6 14.0 %copy-start.7 = (bf16[1,32,3,8192]{3,1,2,0:T(8,128)(2,1)S(1)}, bf16[1,32,3,8192]{3,1,2,0:T(8,128)(2,1)}, u32[]{:S(2)}) copy-start(bf16[1,32,3,8192]{3,1,2,0:T(8,128)(2,1)} %param.8) | copy-start | bytes 4718596
  3.1 28.3 %all-to-all-start.1 = ((bf16[32,1,64,128]{3,0,1,2:T(8,128)(2,1)}), bf16[32,1,64,128]{3,0,1,2:T(8,128)(2,1)S(1)}, u32[]{:S(2)}, u32[]{:S(2)}) async-start(bf16[32,1,64,128]{3,0,1,2:T(8,128)(2,1)} %copy.303), calls=%async_computation.1 | async-start | bytes 1048576 | tf_op jit(solution)/shard_map/all_to_all | solution.py:28
  31.3 0.8 copy-start.4
  32.1 46.0 %all-to-all-start = ((bf16[32,3,64,128]{3,0,1,2:T(8,128)(2,1)}), bf16[32,3,64,128]{3,0,1,2:T(8,128)(2,1)}, u32[]{:S(2)}, u32[]{:S(2)}) async-start(bf16[32,3,64,128]{3,0,1,2:T(8,128)(2,1)} %copy.300), calls=%async_computation | async-start | bytes 3145728 | tf_op jit(solution)/shard_map/all_to_all | solution.py:27
  43.3 2.4 copy-start.5
  79.8 1.3 copy-start.2
  89.9 4.0 %copy-start = (f32[512,5120]{1,0:T(8,128)}, f32[512,5120]{1,0:T(8,128)S(1)}, u32[]{:S(2)}) copy-start(f32[512,5120]{1,0:T(8,128)S(1)} %get-tuple-element.320) | copy-start | bytes 31457284 | tf_op jit(solution)/shard_map/while
  93.9 1.6 copy-start.10
  95.5 7.9 %copy-start.1 = (f32[512,5120]{1,0:T(8,128)S(1)}, f32[512,5120]{1,0:T(8,128)}, u32[]{:S(2)}) copy-start(f32[512,5120]{1,0:T(8,128)} %copy-done) | copy-start | bytes 31457284 | tf_op jit(solution)/shard_map/while
  95.5 7.9 %copy-start.9 = (bf16[5120,1,128]{2,0,1:T(8,128)(2,1)S(1)}, bf16[5120,1,128]{2,0,1:T(8,128)(2,1)}, u32[]{:S(2)}) copy-start(bf16[5120,1,128]{2,0,1:T(8,128)(2,1)} %get-tuple-element.360) | copy-start | bytes 3932164 | tf_op jit(solution)/shard_map/while
  110.2 2.5 copy-start.8
  122.0 4.0 %copy-start = (f32[512,5120]{1,0:T(8,128)}, f32[512,5120]{1,0:T(8,128)S(1)}, u32[]{:S(2)}) copy-start(f32[512,5120]{1,0:T(8,128)S(1)} %get-tuple-element.320) | copy-start | bytes 31457284 | tf_op jit(solution)/shard_map/while
  126.0 1.6 copy-start.10
  127.6 8.7 %copy-start.1 = (f32[512,5120]{1,0:T(8,128)S(1)}, f32[512,5120]{1,0:T(8,128)}, u32[]{:S(2)}) copy-start(f32[512,5120]{1,0:T(8,128)} %copy-done) | copy-start | bytes 31457284 | tf_op jit(solution)/shard_map/while
  127.6 8.7 %copy-start.9 = (bf16[5120,1,128]{2,0,1:T(8,128)(2,1)S(1)}, bf16[5120,1,128]{2,0,1:T(8,128)(2,1)}, u32[]{:S(2)}) copy-start(bf16[5120,1,128]{2,0,1:T(8,128)(2,1)} %get-tuple-element.360) | copy-start | bytes 3932164 | tf_op jit(solution)/shard_map/while
  143.0 2.5 copy-start.8
  154.8 4.0 %copy-start = (f32[512,5120]{1,0:T(8,128)}, f32[512,5120]{1,0:T(8,128)S(1)}, u32[]{:S(2)}) copy-start(f32[512,5120]{1,0:T(8,128)S(1)} %get-tuple-element.320) | copy-start | bytes 31457284 | tf_op jit(solution)/shard_map/while
  158.8 1.6 copy-start.10
  160.4 8.7 %copy-start.1 = (f32[512,5120]{1,0:T(8,128)S(1)}, f32[512,5120]{1,0:T(8,128)}, u32[]{:S(2)}) copy-start(f32[512,5120]{1,0:T(8,128)} %copy-done) | copy-start | bytes 31457284 | tf_op jit(solution)/shard_map/while
  160.4 8.7 %copy-start.9 = (bf16[5120,1,128]{2,0,1:T(8,128)(2,1)S(1)}, bf16[5120,1,128]{2,0,1:T(8,128)(2,1)}, u32[]{:S(2)}) copy-start(bf16[5120,1,128]{2,0,1:T(8,128)(2,1)} %get-tuple-element.360) | copy-start | bytes 3932164 | tf_op jit(solution)/shard_map/while
  175.8 2.5 copy-start.8
  187.7 4.0 %copy-start = (f32[512,5120]{1,0:T(8,128)}, f32[512,5120]{1,0:T(8,128)S(1)}, u32[]{:S(2)}) copy-start(f32[512,5120]{1,0:T(8,128)S(1)} %get-tuple-element.320) | copy-start | bytes 31457284 | tf_op jit(solution)/shard_map/while
  191.6 1.6 copy-start.10
  193.2 8.7 %copy-start.1 = (f32[512,5120]{1,0:T(8,128)S(1)}, f32[512,5120]{1,0:T(8,128)}, u32[]{:S(2)}) copy-start(f32[512,5120]{1,0:T(8,128)} %copy-done) | copy-start | bytes 31457284 | tf_op jit(solution)/shard_map/while
  193.2 8.7 %copy-start.9 = (bf16[5120,1,128]{2,0,1:T(8,128)(2,1)S(1)}, bf16[5120,1,128]{2,0,1:T(8,128)(2,1)}, u32[]{:S(2)}) copy-start(bf16[5120,1,128]{2,0,1:T(8,128)(2,1)} %get-tuple-element.360) | copy-start | bytes 3932164 | tf_op jit(solution)/shard_map/while
  208.7 2.5 copy-start.8
  217.5 2.5 copy-start.6
  267.9 37.7 %collective-permute-start = (bf16[32,3,64,128]{3,2,1,0:T(8,128)(2,1)S(1)}, bf16[32,3,64,128]{3,2,1,0:T(8,128)(2,1)S(1)}, u32[]{:S(2)}, u32[]{:S(2)}) collective-permute-start(bf16[32,3,64,128]{3,2,1,0:T(8,128)(2,1)S(1)} %copy.372), channel_id=1, source_target_pairs={{64,0},{128,64},{192,128},{0,192},{65,1},{129,65},{193,129},{1,193... | collective-permute-start | bytes 4718600 | tf_op jit(solution)/shard_map/ppermute | solution.py:14
  268.8 1.9 copy-start.3
  268.8 2.4 slice-start
